TPU v7x, 256 devices: a whole 4x4x8 slice. The times are simulated.
256 devices in a mesh: row: 32 (over y, z_lo, core), col: 8 (over x, z_hi).
Axes of the slice: x: 4, y: 4, z: 8 (z_hi: 2, z_lo: 4; z = z_hi * 4 + z_lo), core: 2. Of those that a mesh axis runs over, the one named last changes fastest.
Arguments:
- features: bfloat16 [32768, 512], P(('row', 'col')), may hold values from -6 to 6
- edge_tiles: bfloat16 [8192, 128, 128], P(('row', 'col')), may hold values from 0 to 1
- tile_rows: int32 [256, 32], P(('row', 'col')), may hold values from 0 to 7
- tile_cols: int32 [256, 32], P(('row', 'col')), may hold values from 0 to 31
- tile_count: int32 [256], P(('row', 'col')), may hold values from 8 to 32, as said below
- node_order: int32 [256, 128], P(('row', 'col')), may hold values from 0 to 127, each once within a row
- w_self: bfloat16 [512, 512], replicated, may hold values from -0.25 to 0.25
- w_neigh: bfloat16 [512, 512], replicated, may hold values from -12 to 12
- bias_term: bfloat16 [512], replicated, may hold values from -3 to 3
- cotangent: bfloat16 [32768, 512], P(('row', 'col')), may hold values from -6 to 6
Outputs:
- activations: bfloat16 [32768, 512], P(('row', 'col'))
- feature_grad: float32 [32768, 512], P(('row', 'col'))
- self_grad: float32 [512, 512], replicated
- neigh_grad: float32 [512, 512], replicated
- bias_grad: float32 [512], replicated
Inputs may be any that keep to these rules, and one draw needn't show every extreme that they name: Only the first tile_count[b] slots of block b's tile list are valid; later slots are padding and are ignored. The busiest block holds 32 tiles and the lightest 32 // 4. `tile_rows`: tile coordinates may repeat within a block's list. `tile_cols`: tile coordinates may repeat within a block's list.
All inputs are finite; a program needn't handle non-finite values.
Results may differ from a plain program's by a relative error of at most 0.0042.
Values may be sent and summed in bfloat16 or wider, within the bound.
A program may use at most 64 MiB of HBM per device.

v0:
```python
import math

import jax
import jax.numpy as jnp
from jax import lax
from jax.sharding import PartitionSpec as P


def forward_tiles(edge_tiles, rows_at, cols_at, live_mask, column, row_tiles):
    tile_total, tile_size, _ = edge_tiles.shape
    channels = column.shape[1]
    col_blocks = column.reshape(-1, tile_size, channels)
    step_size = math.gcd(tile_total, 16)

    def forward_advance(step_index, carry):
        summed, degree = carry
        offset = step_index * step_size
        tile_group = lax.dynamic_slice_in_dim(edge_tiles, offset, step_size, 0)
        where_rows = lax.dynamic_slice_in_dim(rows_at, offset, step_size, 0)
        where_cols = lax.dynamic_slice_in_dim(cols_at, offset, step_size, 0)
        weights = lax.dynamic_slice_in_dim(live_mask, offset, step_size, 0)
        picked = col_blocks[where_cols]
        products = jnp.einsum(
            "tij,tjf->tif", tile_group, picked, preferred_element_type=jnp.float32
        )
        row_sums = jnp.sum(tile_group.astype(jnp.float32), axis=2)
        summed = summed.at[where_rows].add(products * weights[:, None, None])
        degree = degree.at[where_rows].add(row_sums * weights[:, None])
        return (summed, degree)

    start_sums = (
        jnp.zeros((row_tiles, tile_size, channels), jnp.float32),
        jnp.zeros((row_tiles, tile_size), jnp.float32),
    )
    return lax.fori_loop(0, tile_total // step_size, forward_advance, start_sums)


def backward_tiles(edge_tiles, rows_at, cols_at, live_mask, row_grads, col_tiles):
    tile_total, tile_size, _ = edge_tiles.shape
    channels = row_grads.shape[1]
    row_blocks = row_grads.reshape(-1, tile_size, channels)
    step_size = math.gcd(tile_total, 16)

    def backward_advance(step_index, summed):
        offset = step_index * step_size
        tile_group = lax.dynamic_slice_in_dim(edge_tiles, offset, step_size, 0)
        where_rows = lax.dynamic_slice_in_dim(rows_at, offset, step_size, 0)
        where_cols = lax.dynamic_slice_in_dim(cols_at, offset, step_size, 0)
        weights = lax.dynamic_slice_in_dim(live_mask, offset, step_size, 0)
        picked = row_blocks[where_rows]
        products = jnp.einsum(
            "tij,tif->tjf", tile_group, picked, preferred_element_type=jnp.float32
        )
        return summed.at[where_cols].add(products * weights[:, None, None])

    return lax.fori_loop(
        0,
        tile_total // step_size,
        backward_advance,
        jnp.zeros((col_tiles, tile_size, channels), jnp.float32),
    )


def times_transposed(left, right):
    return lax.dot_general(
        left, right, (((1,), (1,)), ((), ())), preferred_element_type=jnp.float32
    )


def shards(
    features,
    edge_tiles,
    tile_rows,
    tile_cols,
    tile_count,
    node_order,
    w_self,
    w_neigh,
    bias_term,
    cotangent,
):
    ordering = node_order[0]
    own_rows = features[ordering]
    node_dev = own_rows.shape[0]
    channels = own_rows.shape[1]
    tile_size = edge_tiles.shape[1]
    tile_total = edge_tiles.shape[0]
    col_count = lax.axis_size("col")
    row_count = lax.axis_size("row")
    live_mask = (jnp.arange(tile_total) < tile_count[0]).astype(jnp.float32)
    rows_at = tile_rows[0]
    cols_at = tile_cols[0]
    column = lax.all_gather(own_rows, "row", axis=0, tiled=True)
    summed, degree = forward_tiles(
        edge_tiles, rows_at, cols_at, live_mask, column, col_count * node_dev // tile_size
    )
    summed = summed.reshape(col_count * node_dev, channels)
    degree = degree.reshape(col_count * node_dev)
    own_sum, own_degree = (
        lax.psum_scatter(summed, "col", scatter_dimension=0, tiled=True),
        lax.psum_scatter(degree, "col", scatter_dimension=0, tiled=True),
    )
    inverse_degree = 1.0 / (1.0 + own_degree)
    neigh_mean = (own_sum * inverse_degree[:, None]).astype(jnp.bfloat16)
    preact = (
        jnp.dot(own_rows, w_self, preferred_element_type=jnp.float32)
        + jnp.dot(neigh_mean, w_neigh, preferred_element_type=jnp.float32)
        + bias_term.astype(jnp.float32)
    )
    activations = (jnp.maximum(preact, 0.0) + jnp.expm1(jnp.minimum(preact, 0.0))).astype(
        jnp.bfloat16
    )
    grad_pre = (cotangent.astype(jnp.float32) * jnp.exp(jnp.minimum(preact, 0.0))).astype(
        jnp.bfloat16
    )
    self_part = lax.dot_general(
        own_rows, grad_pre, (((0,), (0,)), ((), ())), preferred_element_type=jnp.float32
    )
    neigh_part = lax.dot_general(
        neigh_mean, grad_pre, (((0,), (0,)), ((), ())), preferred_element_type=jnp.float32
    )
    bias_part = jnp.sum(grad_pre.astype(jnp.float32), axis=0)
    self_grad, neigh_grad, bias_grad = lax.psum((self_part, neigh_part, bias_part), ("row", "col"))
    own_agg = (times_transposed(grad_pre, w_neigh) * inverse_degree[:, None]).astype(jnp.bfloat16)
    row_grads = lax.all_gather(own_agg, "col", axis=0, tiled=True)
    col_terms = backward_tiles(
        edge_tiles, rows_at, cols_at, live_mask, row_grads, row_count * node_dev // tile_size
    )
    own_grad = lax.psum_scatter(
        col_terms.reshape(row_count * node_dev, channels), "row", scatter_dimension=0, tiled=True
    )
    local_grad = times_transposed(grad_pre, w_self) + own_grad
    feature_grad = jnp.zeros_like(local_grad).at[ordering].set(local_grad)
    return (activations, feature_grad, self_grad, neigh_grad, bias_grad)


def solution(mesh):
    placed = (
        P(("row", "col"), None),
        P(("row", "col"), None, None),
        P(("row", "col"), None),
        P(("row", "col"), None),
        P(("row", "col")),
        P(("row", "col"), None),
        P(),
        P(),
        P(),
        P(("row", "col"), None),
    )
    return jax.shard_map(
        shards,
        mesh=mesh,
        in_specs=placed,
        out_specs=(P(("row", "col"), None), P(("row", "col"), None), P(), P(), P()),
        check_vma=False,
    )
```

profile of v0, /device:TPU:2, one launch (start us, length us, event | category | flops | bytes accessed | tf_op | source)
XLA Modules:
  0.0 742.1 jit_solution(8785978623316834144)
XLA Ops:
  7.2 0.7 fusion.11
  7.9 2.4 gather_fusion.2
  11.1 64.9 %all-gather.6.cloned.1.call-done = bf16[4096,512]{1,0:T(8,128)(2,1)} async-done(((bf16[128,512]{1,0:T(8,128)(2,1)}), bf16[4096,512]{1,0:T(8,128)(2,1)}) %all-gather.6.cloned.1.call-update) | async-done | bytes 4194320 | tf_op jit(solution)/shard_map/all_gather | solution.py:93
  76.0 0.2 broadcast_in_dim.52
  76.3 35.4 %while.28 = (s32[]{:T(128)}, f32[8,128,512]{2,1,0:T(8,128)S(1)}, f32[8,128]{1,0:T(8,128)S(1)}, s32[32]{0:T(128)}, bf16[32,128,128]{2,1,0:T(8,128)(2,1)}, /*index...) while((s32[]{:T(128)}, f32[8,128,512]{2,1,0:T(8,128)S(1)}, ...), condition=%wide.region_4.0_spmd, body=%wide.region_0.0_spmd.sunk | while | flops 271060064 | bytes 24143164 | solution.py:35
  76.4 0.8 compare_select_fusion.7
  77.2 4.3 gather_fusion
  81.4 0.1 dynamic_slice.75
  81.5 4.4 convolution_multiply_fusion.5
  85.9 6.1 scatter_fusion
  92.1 1.3 convert_reduce_fusion.3
  93.4 0.7 scatter_custom_fusion.12
  94.1 0.8 compare_select_fusion.7
  94.8 4.3 gather_fusion
  99.2 4.4 convolution_multiply_fusion.5
  103.6 6.2 scatter_fusion
  109.8 1.3 convert_reduce_fusion.3
  111.0 0.7 scatter_custom_fusion.12
  111.8 1.3 copy-done.1
  113.2 0.6 dynamic-slice
  114.5 0.2 fusion.14
  114.7 28.1 %all-reduce = f32[1024]{0:T(1024)S(1)} all-reduce(f32[1024]{0:T(1024)S(1)} %bitcast.36), channel_id=4, replica_groups=mesh['row'=32,'col'=8] {'col'}, use_global_device_ids=true, to_apply=%region_6.0.clone | all-reduce | flops 1024 | bytes 8192
  142.8 0.1 fusion.12
  142.8 65.3 %reduce-scatter.3.cloned.1.call-done = f32[128,512]{1,0:T(8,128)} async-done(((f32[1024,512]{1,0:T(8,128)}), f32[128,512]{1,0:T(8,128)}) %reduce-scatter.3.cloned.1.call-update) | async-done | bytes 262160 | tf_op jit(solution)/shard_map/reduce_scatter | solution.py:100
  208.1 2.0 convert_reduce_fusion.1
  210.1 1.0 fusion.8
  211.2 57.7 %all-gather.4.cloned.1.call-done = bf16[1024,512]{1,0:T(8,128)(2,1)} async-done(((bf16[128,512]{1,0:T(8,128)(2,1)}), bf16[1024,512]{1,0:T(8,128)(2,1)}) %all-gather.4.cloned.1.call-update) | async-done | bytes 1048592 | tf_op jit(solution)/shard_map/all_gather | solution.py:125
  268.9 4.3 broadcast_in_dim.54
  273.2 30.9 %while.29 = (s32[]{:T(128)}, f32[32,128,512]{2,1,0:T(8,128)}, s32[32]{0:T(128)S(1)}, bf16[32,128,128]{2,1,0:T(8,128)(2,1)}, s32[32]{0:T(128)S(1)}, /*index=5*/bf...) while((s32[]{:T(128)}, f32[32,128,512]{2,1,0:T(8,128)}, ...), condition=%wide.region_9.0_spmd, body=%wide.region_7.9_spmd.sunk | while | flops 270533728 | bytes 23597872 | solution.py:56
  273.2 0.1 compare_select_fusion.8
  273.3 1.9 gather_fusion.1
  275.2 0.1 dynamic_slice.78
  275.3 3.9 convolution_multiply_fusion.6
  279.1 9.5 %scatter_fusion.1 = f32[32,128,512]{2,1,0:T(8,128)} fusion(f32[32,128,512]{2,1,0:T(8,128)} %get-tuple-element.473, s32[16]{0:T(128)S(1)} %get-tuple-element.423, f32[16,128,512]{2,1,0:T(8,128)} %convolution_multiply_fusion.6), kind=kCustom, calls=%fused_computation.5.clone.1 | custom fusion | flops 1048576 | bytes 12582976 | tf_op jit(solution)/shard_map/while/body/eval_jaxpr/scatter-add | solution.py:54
  288.7 0.1 compare_select_fusion.8
  288.7 1.9 gather_fusion.1
  290.7 0.1 dynamic_slice.78
  290.7 3.9 convolution_multiply_fusion.6
  294.6 9.5 %scatter_fusion.1 = f32[32,128,512]{2,1,0:T(8,128)} fusion(f32[32,128,512]{2,1,0:T(8,128)} %get-tuple-element.473, s32[16]{0:T(128)S(1)} %get-tuple-element.423, f32[16,128,512]{2,1,0:T(8,128)} %convolution_multiply_fusion.6), kind=kCustom, calls=%fused_computation.5.clone.1 | custom fusion | flops 1048576 | bytes 12582976 | tf_op jit(solution)/shard_map/while/body/eval_jaxpr/scatter-add | solution.py:54
  304.1 1.3 fusion.15
  305.4 1.4 fusion.13
  306.8 75.2 %psum.23 = f32[512]{0:T(512)} all-reduce(f32[512]{0:T(512)S(1)} %get-tuple-element.318), channel_id=1, replica_groups=mesh['row'=32,'col'=8] {'row','col'}, use_global_device_ids=true, to_apply=%region_15.0 | all-reduce | flops 512 | bytes 4096 | tf_op jit(solution)/shard_map/psum | solution.py:123
  382.0 81.6 %reduce-scatter.5.cloned.1.call-done = f32[128,512]{1,0:T(8,128)} async-done(((f32[4096,512]{1,0:T(8,128)}), f32[128,512]{1,0:T(8,128)}) %reduce-scatter.5.cloned.1.call-update) | async-done | bytes 262160 | tf_op jit(solution)/shard_map/reduce_scatter | solution.py:129
  463.7 1.3 convolution_add_fusion
  464.9 1.7 scatter_custom_fusion.3
  466.6 264.4 %all-reduce.4.cloned.1.call-done = (f32[512,512]{1,0:T(8,128)}, f32[512,512]{1,0:T(8,128)}) async-done(((f32[512,512]{1,0:T(8,128)}, f32[512,512]{1,0:T(8,128)}), (f32[512,512]{1,0:T(8,128)}, f32[512,512]{1,0:T(8,128)})) %all-reduce.4.cloned.1.call-update) | async-done | bytes 2097168 | tf_op jit(solution)/shard_map/psum | solution.py:123
  731.0 2.3 copy.39
  733.3 2.3 copy.40
  (38 shorter events, 0.5 us)
Async XLA Ops:
  7.2 201.0 %copy-start = (bf16[512,512]{1,0:T(8,128)(2,1)S(1)}, bf16[512,512]{1,0:T(8,128)(2,1)}, u32[]{:S(2)}) copy-start(bf16[512,512]{1,0:T(8,128)(2,1)} %param.21) | copy-start | bytes 1572868
  7.2 68.8 %all-gather.6.cloned.1.call-start = ((), (), s32[]{:S(2)}) async-start(), calls=%async_computation.5 | async-start | bytes 4325376 | tf_op jit(solution)/shard_map/all_gather | solution.py:93
  10.4 197.7 %reduce-scatter.3.cloned.1.call-start = ((), (), s32[]{:S(2)}) async-start(), calls=%async_computation.2 | async-start | bytes 2359296 | tf_op jit(solution)/shard_map/reduce_scatter | solution.py:100
  76.3 36.9 %copy-start.8 = (bf16[512]{0:T(512)(128)(2,1)S(1)}, bf16[512]{0:T(512)(128)(2,1)}, u32[]{:S(2)}) copy-start(bf16[512]{0:T(512)(128)(2,1)} %param.22) | copy-start | bytes 3076
  76.3 36.9 %copy-start.9 = (u32[256]{0:T(256)S(1)}, u32[256]{0:T(256)}, u32[]{:S(2)}) copy-start(u32[256]{0:T(256)} %constant.100) | copy-start | bytes 3076
  76.3 38.2 %copy-start.2 = (bf16[128,512]{1,0:T(8,128)(2,1)S(1)}, bf16[128,512]{1,0:T(8,128)(2,1)}, u32[]{:S(2)}) copy-start(bf16[128,512]{1,0:T(8,128)(2,1)} %gather_fusion.2) | copy-start | bytes 393220
  76.3 38.2 %copy-start.3 = (bf16[512,512]{1,0:T(8,128)(2,1)S(1)}, bf16[512,512]{1,0:T(8,128)(2,1)}, u32[]{:S(2)}) copy-start(bf16[512,512]{1,0:T(8,128)(2,1)} %param.20) | copy-start | bytes 1572868
  76.3 131.8 %copy-start.5 = (bf16[128,512]{1,0:T(8,128)(2,1)S(1)}, bf16[128,512]{1,0:T(8,128)(2,1)}, u32[]{:S(2)}) copy-start(bf16[128,512]{1,0:T(8,128)(2,1)} %param.23) | copy-start | bytes 393220
  111.8 1.3 copy-start.1
  113.1 155.8 %all-gather.4.cloned.1.call-start = ((), (), s32[]{:S(2)}) async-start(), calls=%async_computation.3 | async-start | bytes 1179648 | tf_op jit(solution)/shard_map/all_gather | solution.py:125
  211.1 252.5 %reduce-scatter.5.cloned.1.call-start = ((), (), s32[]{:S(2)}) async-start(), calls=%async_computation.4 | async-start | bytes 8650752 | tf_op jit(solution)/shard_map/reduce_scatter | solution.py:129
  268.9 4.3 copy-start.6
  268.9 4.3 copy-start.7
  304.0 1.4 copy-start.4
  304.1 426.9 %all-reduce.4.cloned.1.call-start = ((), (), s32[]{:S(2)}) async-start(), calls=%async_computation.6 | async-start | bytes 4194304 | tf_op jit(solution)/shard_map/psum | solution.py:123
Sparse Core Ops, SparseCore 0:
  10.5 65.4 all-gather.5
  113.2 94.8 reduce-scatter.2
  211.3 57.5 all-gather.3
  304.2 159.4 reduce-scatter.4
  469.7 261.3 all-reduce.3
where the time goes:
time: 743 us; the launch traced here: 742 us
  waiting for transfers between devices  534 us (72%)
  blocking collectives  103 us (14%)
  other arithmetic  37.8 us (5%)
  local copies, waits for them, and re-layouts  27.8 us (4%)
  matrix products  23.6 us (3%)
  between operations  15.2 us (2%)
    psum x1, waiting for transfers between devices, shards(): lax.psum((self_part, neigh_part, bias_part), ('row', 'col'))  264 us
    reduce_scatter x1, waiting for transfers between devices, shards(): lax.psum_scatter(col_terms.reshape(row_count * node_dev, channels), 'row'...  81.6 us
    psum x1, blocking collectives, shards(): lax.psum((self_part, neigh_part, bias_part), ('row', 'col'))  75.2 us
    reduce_scatter x1, waiting for transfers between devices, shards(): lax.psum_scatter(summed, 'col', scatter_dimension=0, tiled=True)  65.3 us
    all_gather x1, waiting for transfers between devices, shards(): column = lax.all_gather(own_rows, 'row', axis=0, tiled=True)  64.9 us
    all_gather x1, waiting for transfers between devices, shards(): row_grads = lax.all_gather(own_agg, 'col', axis=0, tiled=True)  57.7 us
    unnamed x1, blocking collectives  28.1 us
    scatter-add x2, other arithmetic, backward_advance(): return summed.at[where_cols].add(products * weights[:, None, None])  19 us
  transfers between devices with their start and end apart: 5, of which 5 were waited for; matrix products, arithmetic and copies ran while one was open for 1% of the time, Pallas kernels for 0%

commit v1 on v0

v1 whole, which is shorter than its diff:
```python
import functools

import jax
import jax.numpy as jnp
from jax import lax
from jax.experimental import pallas as pl
from jax.experimental.pallas import tpu as pltpu
from jax.sharding import PartitionSpec as P

LINE = 4
CORES = 2
HALVES = 2
ROWS = LINE * LINE * CORES
COLS = LINE * HALVES
F32 = jnp.float32
BF16 = jnp.bfloat16


def row_place():
    me = lax.axis_index("row")
    return me // (LINE * CORES), (me // CORES) % LINE, me % CORES


def row_of(y, z, core):
    return (y * LINE + z) * CORES + core


def z_partners(z):
    return (z + 1 - 2 * (z % 2), (z + 2) % LINE, LINE - 1 - z)


def greet(targets):
    barrier = pltpu.get_barrier_semaphore()
    for target in targets:
        pl.semaphore_signal(barrier, inc=1, device_id=target, device_id_type=pl.DeviceIdType.MESH)
    pl.semaphore_wait(barrier, len(targets))


def start_copy(source, target, send_sem, recv_sem, device):
    copy = pltpu.make_async_remote_copy(
        src_ref=source,
        dst_ref=target,
        send_sem=send_sem,
        recv_sem=recv_sem,
        device_id=device,
        device_id_type=pl.DeviceIdType.MESH,
    )
    copy.start()
    return copy


def arrived(target, recv_sem):
    pltpu.make_async_copy(target, target, recv_sem).wait()


def one_hot_order(order_ref, size):
    return order_ref[...] == lax.broadcasted_iota(jnp.int32, (size, size), 0)


def gather_kernel(order_ref, feat_ref, column_ref, send_sem, recv_sem, half_sem):
    y, z, core = row_place()
    size = feat_ref.shape[0]
    half = size // 2
    up, down, far = (y + 1) % LINE, (y + LINE - 1) % LINE, (y + 2) % LINE
    along = z_partners(z)
    other = {"row": row_of(y, z, 1 - core)}
    to_up = {"row": row_of(up, z, core)}
    to_down = {"row": row_of(down, z, core)}
    to_along = [{"row": row_of(y, place, core)} for place in along]
    me = row_of(y, z, core)
    chosen = one_hot_order(order_ref, size).astype(F32).astype(BF16)
    column_ref[me] = lax.dot_general(
        chosen, feat_ref[...], (((0,), (0,)), ((), ())), preferred_element_type=F32
    ).astype(BF16)
    greet([other, to_up, to_down, *to_along])
    sent = []

    def push(block, device):
        sent.append(
            start_copy(
                column_ref.at[block], column_ref.at[block], send_sem.at[len(sent)], recv_sem.at[block], device
            )
        )

    def push_half(block, slot, part, device):
        rows = pl.ds(part * half, half)
        sent.append(
            start_copy(
                column_ref.at[block, rows],
                column_ref.at[block, rows],
                send_sem.at[len(sent)],
                half_sem.at[slot, part],
                device,
            )
        )

    def wait_block(block):
        arrived(column_ref.at[block], recv_sem.at[block])

    def from_line(index):
        block = row_of(y, along[index], core)
        wait_block(block)
        push(block, to_up)
        push(block, to_down)
        push(block, other)

    places = (z, *along)

    def from_ring(index):
        below, above = row_of(down, places[index], core), row_of(up, places[index], core)
        wait_block(below)
        push_half(below, index, 0, to_up)
        push(below, other)
        wait_block(above)
        push_half(above, index, 1, to_down)
        push(above, other)

    def from_far(index):
        block = row_of(far, places[index], core)
        for part in range(2):
            arrived(column_ref.at[block, pl.ds(part * half, half)], half_sem.at[index, part])
        push(block, other)

    push(me, to_up)
    push(me, to_down)
    for device in to_along:
        push(me, device)
    push(me, other)
    from_line(0)
    from_ring(0)
    from_line(1)
    from_ring(1)
    from_line(2)
    from_far(0)
    from_ring(2)
    from_far(1)
    from_ring(3)
    from_far(2)
    from_far(3)
    for place in range(LINE * LINE):
        wait_block(place * CORES + 1 - core)
    for copy in sent:
        copy.wait_send()


def gather_rows(order, features):
    size, channels = features.shape
    return pl.pallas_call(
        gather_kernel,
        out_shape=jax.ShapeDtypeStruct((ROWS, size, channels), BF16),
        in_specs=[pl.BlockSpec(memory_space=pltpu.VMEM)] * 2,
        out_specs=pl.BlockSpec(memory_space=pltpu.VMEM),
        scratch_shapes=[
            pltpu.SemaphoreType.DMA((35,)),
            pltpu.SemaphoreType.DMA((ROWS,)),
            pltpu.SemaphoreType.DMA((LINE, 2)),
        ],
        compiler_params=pltpu.CompilerParams(collective_id=0, has_side_effects=True),
        name="gather_rows",
    )(order, features)


def forward_kernel(count_ref, rows_ref, cols_ref, tiles_ref, column_ref, sums_ref, degree_ref):
    size = tiles_ref.shape[1]
    sums_ref[...] = jnp.zeros_like(sums_ref)
    degree_ref[...] = jnp.zeros_like(degree_ref)
    ones = jnp.ones((8, size), BF16)

    def advance(slot, carry):
        at = rows_ref[0, slot]
        tile = tiles_ref[slot]
        sums_ref[at] += jnp.dot(tile, column_ref[cols_ref[0, slot]], preferred_element_type=F32)
        degree_ref[at] += lax.dot_general(
            ones, tile, (((1,), (1,)), ((), ())), preferred_element_type=F32
        )
        return carry

    lax.fori_loop(0, count_ref[0], advance, 0)


def forward_sums(count, rows_at, cols_at, tiles, column):
    _, size, channels = column.shape
    return pl.pallas_call(
        forward_kernel,
        out_shape=(
            jax.ShapeDtypeStruct((COLS, size, channels), F32),
            jax.ShapeDtypeStruct((COLS, 8, size), F32),
        ),
        in_specs=[pl.BlockSpec(memory_space=pltpu.SMEM)] * 3 + [pl.BlockSpec(memory_space=pltpu.VMEM)] * 2,
        out_specs=(pl.BlockSpec(memory_space=pltpu.VMEM),) * 2,
        name="forward_sums",
    )(count, rows_at, cols_at, tiles, column)


def middle_kernel(
    sums_ref,
    degree_ref,
    own_ref,
    w_self_ref,
    w_neigh_ref,
    bias_ref,
    cot_ref,
    act_ref,
    grad_ref,
    self_ref,
    neigh_ref,
    bias_grad_ref,
    agg_ref,
    far_out,
    near_out,
    mixed_out,
    cross_out,
    far_in,
    near_in,
    mixed_in,
    cross_in,
    degree_in,
    send_sem,
    far_sem,
    near_sem,
    mixed_sem,
    cross_sem,
    degree_sem,
    agg_sem,
    agg_half_sem,
):
    here = lax.axis_index("col")
    x, side = here // HALVES, here % HALVES
    size = own_ref.shape[0]
    half = size // 2
    low, high = pl.ds(0, half), pl.ds(half, half)
    up, down, far = (x + 1) % LINE, (x + LINE - 1) % LINE, (x + 2) % LINE
    sides = (1 - side, side)

    def col_of(place, where):
        return place * HALVES + where

    to_up = {"col": col_of(up, side)}
    to_down = {"col": col_of(down, side)}
    to_cross = {"col": col_of(x, 1 - side)}
    peers = [to_up, to_down, to_cross, {"col": col_of(far, side)}]
    peers += [{"col": col_of(place, 1 - side)} for place in (up, down, far)]
    sent = []

    def push(source, target, recv_sem, device):
        sent.append(start_copy(source, target, send_sem.at[len(sent)], recv_sem, device))

    greet(peers)
    for offset in range(1, COLS):
        owner = (here + offset) % COLS
        push(degree_ref.at[owner], degree_in.at[offset], degree_sem.at[offset], {"col": owner})
    for phase in range(2):
        block = col_of(far, sides[phase])
        far_out[phase] = sums_ref[block].astype(BF16)
        push(far_out.at[phase, low], far_in.at[phase, 0], far_sem.at[phase, 0], to_up)
        push(far_out.at[phase, high], far_in.at[phase, 1], far_sem.at[phase, 1], to_down)
        near_out[phase, 0] = sums_ref[col_of(up, sides[phase]), high].astype(BF16)
        near_out[phase, 1] = sums_ref[col_of(down, sides[phase]), low].astype(BF16)
        push(near_out.at[phase, 0], near_in.at[phase, 0], near_sem.at[phase, 0], to_up)
        push(near_out.at[phase, 1], near_in.at[phase, 1], near_sem.at[phase, 1], to_down)
    own = own_ref[...]
    self_term = jnp.dot(own, w_self_ref[...], preferred_element_type=F32) + bias_ref[...].astype(F32)

    def gathered(phase):
        arrived(far_in.at[phase, 0], far_sem.at[phase, 0])
        mixed_out[phase, 0] = (
            sums_ref[col_of(up, sides[phase]), low] + far_in[phase, 0].astype(F32)
        ).astype(BF16)
        push(mixed_out.at[phase, 0], mixed_in.at[phase, 0], mixed_sem.at[phase, 0], to_up)
        arrived(far_in.at[phase, 1], far_sem.at[phase, 1])
        mixed_out[phase, 1] = (
            sums_ref[col_of(down, sides[phase]), high] + far_in[phase, 1].astype(F32)
        ).astype(BF16)
        push(mixed_out.at[phase, 1], mixed_in.at[phase, 1], mixed_sem.at[phase, 1], to_down)
        for part in range(2):
            arrived(near_in.at[phase, part], near_sem.at[phase, part])
        for part in range(2):
            arrived(mixed_in.at[phase, part], mixed_sem.at[phase, part])
        mine = sums_ref[col_of(x, sides[phase])]
        upper = mine[:half] + mixed_in[phase, 0].astype(F32) + near_in[phase, 1].astype(F32)
        lower = mine[half:] + near_in[phase, 0].astype(F32) + mixed_in[phase, 1].astype(F32)
        return jnp.concatenate([upper, lower], axis=0)

    cross_out[...] = gathered(0).astype(BF16)
    push(cross_out, cross_in, cross_sem.at[0], to_cross)
    own_sum = gathered(1)
    degree = degree_ref[here]
    for offset in range(1, COLS):
        arrived(degree_in.at[offset], degree_sem.at[offset])
        degree += degree_in[offset]
    inverse = jnp.broadcast_to((1.0 / (1.0 + degree))[:1], (size, size)).T
    inverse = jnp.concatenate([inverse] * (own.shape[1] // size), axis=1)
    arrived(cross_in, cross_sem.at[0])
    own_sum += cross_in[...].astype(F32)
    neigh_mean = (own_sum * inverse).astype(BF16)
    preact = self_term + jnp.dot(neigh_mean, w_neigh_ref[...], preferred_element_type=F32)
    below = jnp.minimum(preact, 0.0)
    slope = cot_ref[...].astype(F32) * jnp.exp(below)
    grad_pre = slope.astype(BF16)
    agg_ref[here] = (
        lax.dot_general(grad_pre, w_neigh_ref[...], (((1,), (1,)), ((), ())), preferred_element_type=F32)
        * inverse
    ).astype(BF16)
    push(agg_ref.at[here], agg_ref.at[here], agg_sem.at[here], to_cross)
    push(agg_ref.at[here], agg_ref.at[here], agg_sem.at[here], to_up)
    push(agg_ref.at[here], agg_ref.at[here], agg_sem.at[here], to_down)
    grad_ref[...] = grad_pre
    bent = jnp.tanh(0.5 * below)
    act_ref[...] = (jnp.maximum(preact, 0.0) + 2.0 * bent / (1.0 - bent)).astype(BF16)

    def round_ring(where, slot):
        from_down, from_up = col_of(down, where), col_of(up, where)
        arrived(agg_ref.at[from_down], agg_sem.at[from_down])
        push(agg_ref.at[from_down, low], agg_ref.at[from_down, low], agg_half_sem.at[slot, 0], to_up)
        arrived(agg_ref.at[from_up], agg_sem.at[from_up])
        push(agg_ref.at[from_up, high], agg_ref.at[from_up, high], agg_half_sem.at[slot, 1], to_down)

    round_ring(side, 0)
    self_ref[...] = lax.dot_general(own, grad_pre, (((0,), (0,)), ((), ())), preferred_element_type=F32)
    cross = col_of(x, 1 - side)
    arrived(agg_ref.at[cross], agg_sem.at[cross])
    push(agg_ref.at[cross], agg_ref.at[cross], agg_sem.at[cross], to_up)
    push(agg_ref.at[cross], agg_ref.at[cross], agg_sem.at[cross], to_down)
    neigh_ref[...] = lax.dot_general(
        neigh_mean, grad_pre, (((0,), (0,)), ((), ())), preferred_element_type=F32
    )
    bias_grad_ref[...] = jnp.sum(grad_pre.astype(F32), axis=0, keepdims=True)
    round_ring(1 - side, 1)
    for slot, where in enumerate((side, 1 - side)):
        block = col_of(far, where)
        arrived(agg_ref.at[block, low], agg_half_sem.at[slot, 0])
        arrived(agg_ref.at[block, high], agg_half_sem.at[slot, 1])
    for copy in sent:
        copy.wait_send()


def middle(sums, degree, own, w_self, w_neigh, bias, cotangent):
    size, channels = own.shape
    half = size // 2
    wide = w_self.shape[0]
    halves = functools.partial(pltpu.VMEM, dtype=BF16)
    return pl.pallas_call(
        middle_kernel,
        out_shape=(
            jax.ShapeDtypeStruct((size, channels), BF16),
            jax.ShapeDtypeStruct((size, channels), BF16),
            jax.ShapeDtypeStruct((wide, wide), F32),
            jax.ShapeDtypeStruct((wide, wide), F32),
            jax.ShapeDtypeStruct((1, wide), F32),
            jax.ShapeDtypeStruct((COLS, size, channels), BF16),
        ),
        in_specs=[pl.BlockSpec(memory_space=pltpu.VMEM)] * 7,
        out_specs=(pl.BlockSpec(memory_space=pltpu.VMEM),) * 6,
        scratch_shapes=[
            halves((2, size, channels)),
            halves((2, 2, half, channels)),
            halves((2, 2, half, channels)),
            halves((size, channels)),
            halves((2, 2, half, channels)),
            halves((2, 2, half, channels)),
            halves((2, 2, half, channels)),
            halves((size, channels)),
            pltpu.VMEM((COLS, 8, size), F32),
            pltpu.SemaphoreType.DMA((30,)),
            pltpu.SemaphoreType.DMA((2, 2)),
            pltpu.SemaphoreType.DMA((2, 2)),
            pltpu.SemaphoreType.DMA((2, 2)),
            pltpu.SemaphoreType.DMA((1,)),
            pltpu.SemaphoreType.DMA((COLS,)),
            pltpu.SemaphoreType.DMA((COLS,)),
            pltpu.SemaphoreType.DMA((2, 2)),
        ],
        compiler_params=pltpu.CompilerParams(collective_id=1, has_side_effects=True),
        name="middle",
    )(sums, degree, own, w_self, w_neigh, bias, cotangent)


def backward_kernel(count_ref, rows_ref, cols_ref, tiles_ref, agg_ref, terms_ref, total):
    total[...] = jnp.zeros_like(total)

    def advance(slot, carry):
        at = cols_ref[0, slot]
        total[at] += lax.dot_general(
            tiles_ref[slot],
            agg_ref[rows_ref[0, slot]],
            (((0,), (0,)), ((), ())),
            preferred_element_type=F32,
        )
        return carry

    lax.fori_loop(0, count_ref[0], advance, 0)

    def put(block, carry):
        terms_ref[block % CORES, block // CORES] = total[block].astype(BF16)
        return carry

    lax.fori_loop(0, ROWS, put, 0)


def backward_terms(count, rows_at, cols_at, tiles, agg):
    _, size, channels = agg.shape
    return pl.pallas_call(
        backward_kernel,
        out_shape=jax.ShapeDtypeStruct((CORES, ROWS // CORES, size, channels), BF16),
        in_specs=[pl.BlockSpec(memory_space=pltpu.SMEM)] * 3 + [pl.BlockSpec(memory_space=pltpu.VMEM)] * 2,
        out_specs=pl.BlockSpec(memory_space=pltpu.VMEM),
        scratch_shapes=[pltpu.VMEM((ROWS, size, channels), F32)],
        name="backward_terms",
    )(count, rows_at, cols_at, tiles, agg)


def scatter_kernel(
    terms_ref,
    grad_ref,
    w_self_ref,
    order_ref,
    out_ref,
    pair_in,
    far_out,
    near_out,
    mixed_out,
    line_out,
    far_in,
    near_in,
    mixed_in,
    line_in,
    send_sem,
    pair_sem,
    far_sem,
    near_sem,
    mixed_sem,
    line_sem,
):
    y, z, core = row_place()
    size = grad_ref.shape[0]
    half = size // 2
    low, high = pl.ds(0, half), pl.ds(half, half)
    up, down, far = (y + 1) % LINE, (y + LINE - 1) % LINE, (y + 2) % LINE
    along = z_partners(z)
    places = (along[2], along[1], along[0], z)
    other = {"row": row_of(y, z, 1 - core)}
    to_up = {"row": row_of(up, z, core)}
    to_down = {"row": row_of(down, z, core)}
    to_along = [{"row": row_of(y, place, core)} for place in along]
    sent = []

    def push(source, target, recv_sem, device):
        sent.append(start_copy(source, target, send_sem.at[len(sent)], recv_sem, device))

    greet([other, to_up, to_down, *to_along])
    for ring in (far, up, down, y):
        for place in places:
            block = ring * LINE + place
            push(terms_ref.at[1 - core, block], pair_in.at[block], pair_sem.at[block], other)

    def paired(ring, place, rows):
        block = ring * LINE + place
        return terms_ref[core, block, rows].astype(F32) + pair_in[block, rows].astype(F32)

    def wait_pair(ring, place):
        block = ring * LINE + place
        arrived(pair_in.at[block], pair_sem.at[block])

    everything = pl.ds(0, size)
    for index, place in enumerate(places):
        wait_pair(far, place)
        far_out[index] = paired(far, place, everything).astype(BF16)
        push(far_out.at[index, low], far_in.at[index, 0], far_sem.at[index, 0], to_up)
        push(far_out.at[index, high], far_in.at[index, 1], far_sem.at[index, 1], to_down)
    for index, place in enumerate(places):
        wait_pair(up, place)
        near_out[index, 0] = paired(up, place, high).astype(BF16)
        push(near_out.at[index, 0], near_in.at[index, 0], near_sem.at[index, 0], to_up)
        wait_pair(down, place)
        near_out[index, 1] = paired(down, place, low).astype(BF16)
        push(near_out.at[index, 1], near_in.at[index, 1], near_sem.at[index, 1], to_down)
        arrived(far_in.at[index, 0], far_sem.at[index, 0])
        mixed_out[index, 0] = (paired(up, place, low) + far_in[index, 0].astype(F32)).astype(BF16)
        push(mixed_out.at[index, 0], mixed_in.at[index, 0], mixed_sem.at[index, 0], to_up)
        arrived(far_in.at[index, 1], far_sem.at[index, 1])
        mixed_out[index, 1] = (paired(down, place, high) + far_in[index, 1].astype(F32)).astype(BF16)
        push(mixed_out.at[index, 1], mixed_in.at[index, 1], mixed_sem.at[index, 1], to_down)
    local = lax.dot_general(
        grad_ref[...], w_self_ref[...], (((1,), (1,)), ((), ())), preferred_element_type=F32
    )

    def gathered(index):
        place = places[index]
        wait_pair(y, place)
        for part in range(2):
            arrived(near_in.at[index, part], near_sem.at[index, part])
        for part in range(2):
            arrived(mixed_in.at[index, part], mixed_sem.at[index, part])
        upper = paired(y, place, low) + mixed_in[index, 0].astype(F32) + near_in[index, 1].astype(F32)
        lower = paired(y, place, high) + near_in[index, 0].astype(F32) + mixed_in[index, 1].astype(F32)
        return jnp.concatenate([upper, lower], axis=0)

    for index in range(LINE - 1):
        line_out[index] = gathered(index).astype(BF16)
        push(line_out.at[index], line_in.at[index], line_sem.at[index], to_along[LINE - 2 - index])
    local += gathered(LINE - 1)
    for index in range(LINE - 1):
        arrived(line_in.at[index], line_sem.at[index])
        local += line_in[index].astype(F32)
    chosen = one_hot_order(order_ref, size).astype(F32).astype(BF16)
    moved = jnp.zeros_like(local)
    rest = local
    for _ in range(3):
        piece = rest.astype(BF16)
        moved += jnp.dot(chosen, piece, preferred_element_type=F32)
        rest -= piece.astype(F32)
    out_ref[...] = moved
    for copy in sent:
        copy.wait_send()


def scatter_rows(terms, grad_pre, w_self, order):
    size, channels = grad_pre.shape
    half = size // 2
    halves = functools.partial(pltpu.VMEM, dtype=BF16)
    return pl.pallas_call(
        scatter_kernel,
        out_shape=jax.ShapeDtypeStruct((size, channels), F32),
        in_specs=[pl.BlockSpec(memory_space=pltpu.VMEM)] * 4,
        out_specs=pl.BlockSpec(memory_space=pltpu.VMEM),
        scratch_shapes=[
            halves((LINE * LINE, size, channels)),
            halves((LINE, size, channels)),
            halves((LINE, 2, half, channels)),
            halves((LINE, 2, half, channels)),
            halves((LINE - 1, size, channels)),
            halves((LINE, 2, half, channels)),
            halves((LINE, 2, half, channels)),
            halves((LINE, 2, half, channels)),
            halves((LINE - 1, size, channels)),
            pltpu.SemaphoreType.DMA((43,)),
            pltpu.SemaphoreType.DMA((LINE * LINE,)),
            pltpu.SemaphoreType.DMA((LINE, 2)),
            pltpu.SemaphoreType.DMA((LINE, 2)),
            pltpu.SemaphoreType.DMA((LINE, 2)),
            pltpu.SemaphoreType.DMA((LINE - 1,)),
        ],
        compiler_params=pltpu.CompilerParams(collective_id=2, has_side_effects=True),
        name="scatter_rows",
    )(terms, grad_pre, w_self, order)


def shards(
    features,
    edge_tiles,
    tile_rows,
    tile_cols,
    tile_count,
    node_order,
    w_self,
    w_neigh,
    bias_term,
    cotangent,
):
    column = gather_rows(node_order, features)
    own = lax.dynamic_index_in_dim(column, lax.axis_index("row"), 0, keepdims=False)
    sums, degree = forward_sums(tile_count, tile_rows, tile_cols, edge_tiles, column)
    activations, grad_pre, self_part, neigh_part, bias_part, agg = middle(
        sums, degree, own, w_self, w_neigh, bias_term[None], cotangent
    )
    self_grad, neigh_grad, bias_grad = lax.psum((self_part, neigh_part, bias_part), ("row", "col"))
    terms = backward_terms(tile_count, tile_rows, tile_cols, edge_tiles, agg)
    feature_grad = scatter_rows(terms, grad_pre, w_self, node_order)
    return (activations, feature_grad, self_grad, neigh_grad, bias_grad[0])


def solution(mesh):
    placed = (
        P(("row", "col"), None),
        P(("row", "col"), None, None),
        P(("row", "col"), None),
        P(("row", "col"), None),
        P(("row", "col")),
        P(("row", "col"), None),
        P(),
        P(),
        P(),
        P(("row", "col"), None),
    )
    return jax.shard_map(
        shards,
        mesh=mesh,
        in_specs=placed,
        out_specs=(P(("row", "col"), None), P(("row", "col"), None), P(), P(), P()),
        check_vma=False,
    )
```

time: 743 us -> 376 us (0.51)
  waiting for transfers between devices: 534 us -> 146 us
  Pallas kernels: 0 us -> 130 us
  other arithmetic: 37.8 us -> 0 us
  blocking collectives: 103 us -> 74.6 us
  matrix products: 23.6 us -> 0 us
  local copies, waits for them, and re-layouts: 27.8 us -> 9.69 us
    reduce_scatter x2 -> x0, waiting for transfers between devices: 147 us -> none  [the longest x1 81.6 us: shards(): lax.psum_scatter(col_terms.reshape(row_count * node_dev, channels), 'row'...]
    pallas_call x0 -> x5, Pallas kernels: none -> 130 us  [the longest x1 46.7 us: middle(): pl.pallas_call(middle_kernel, out_shape=(jax.ShapeDtypeStruct((size, chan...]
    all_gather x2 -> x0, waiting for transfers between devices: 123 us -> none  [the longest x1 64.9 us: shards(): column = lax.all_gather(own_rows, 'row', axis=0, tiled=True)]
    psum x1, waiting for transfers between devices: 264 us -> 146 us  [shards(): lax.psum((self_part, neigh_part, bias_part), ('row', 'col'))]
    scatter-add x6 -> x0, other arithmetic: 32.7 us -> none  [the longest x2 19 us: backward_advance(): return summed.at[where_cols].add(products * weights[:, None, None])]
    unnamed x1 -> x0, blocking collectives: 28.1 us -> none
    dot_general x10 -> x0, matrix products: 23.6 us -> none  [the longest x2 8.85 us: forward_advance(): jnp.einsum('tij,tjf->tif', tile_group, picked, preferred_element_type=jnp...]
    gather x5 -> x0, local copies, waits for them, and re-layouts: 14.8 us -> none  [the longest x2 8.52 us: forward_advance(): picked = col_blocks[where_cols]]
  transfers between devices with their start and end apart: 5 -> 1, of which waited for: 5 -> 1; matrix products, arithmetic and copies ran while one was open for 1% -> 0% of each run, Pallas kernels for 0% -> 12%
where the time goes in v1:
time: 376 us; the launch traced here: 375 us
  waiting for transfers between devices  146 us (39%)
  Pallas kernels  130 us (35%)
  blocking collectives  74.6 us (20%)
  between operations  14.7 us (4%)
  local copies, waits for them, and re-layouts  9.69 us (3%)
    psum x1, waiting for transfers between devices, shards(): lax.psum((self_part, neigh_part, bias_part), ('row', 'col'))  146 us
    psum x1, blocking collectives, shards(): lax.psum((self_part, neigh_part, bias_part), ('row', 'col'))  74.6 us
    pallas_call x1, Pallas kernels, middle(): pl.pallas_call(middle_kernel, out_shape=(jax.ShapeDtypeStruct((size, chan...  46.7 us
    pallas_call x1, Pallas kernels, scatter_rows(): pl.pallas_call(scatter_kernel, out_shape=jax.ShapeDtypeStruct((size, chan...  37 us
    pallas_call x1, Pallas kernels, gather_rows(): pl.pallas_call(gather_kernel, out_shape=jax.ShapeDtypeStruct((ROWS, size,...  34.6 us
  transfers between devices with their start and end apart: 1, of which 1 were waited for; matrix products, arithmetic and copies ran while one was open for 0% of the time, Pallas kernels for 12%

profile of v1, /device:TPU:2, one launch (start us, length us, event | category | flops | bytes accessed | tf_op | source)
XLA Modules:
  0.0 375.4 jit_solution(180027923367144525)
XLA Ops:
  7.2 0.0 all-reduce.3.cloned.1.call-start
  7.9 1.3 broadcast_in_dim.3.bias_ref
  9.1 34.6 %gather_rows.1.column_ref = bf16[32,128,512]{2,1,0:T(8,128)(2,1)} custom-call(s32[1,128]{1,0:T(1,128)} %order_ref.3, bf16[128,512]{1,0:T(8,128)(2,1)} %feat_ref.1), custom_call_target="tpu_custom_call" | custom-call | tf_op jit(solution)/shard_map/gather_rows/pallas_call | solution.py:148
  43.8 1.6 dynamic-slice_bitcast_fusion.own_ref
  45.3 5.5 %forward_sums.1 = (f32[8,128,512]{2,1,0:T(8,128)}, f32[8,8,128]{2,1,0:T(8,128)}) custom-call(s32[1]{0:T(128)S(6)} %copy.21.count_ref, s32[1,32]{1,0:T(1,128)} %rows_ref.3, s32[1,32]{1,0:T(1,128)} %cols_ref.3, bf16[32,128,128]{2,1,0:T(8,128)(2,1)} %tiles_ref.3, bf16[32,128,512]{2,1,0:T(8,128)(2,1)} %gather_rows.1.column_ref), custom_call_target="tpu_custom_call" | custom-call | tf_op jit(solution)/shard_map/forward_sums/pallas_call | solution.py:183
  50.8 46.7 %middle.1 = (bf16[128,512]{1,0:T(8,128)(2,1)}, bf16[128,512]{1,0:T(8,128)(2,1)}, f32[512,512]{1,0:T(8,128)}, f32[512,512]{1,0:T(8,128)}, f32[1,512]{1,0:T(1,128)}, /*index=5*/bf16[8,128,512]{2,1,0:T(8,128)(2,1)}) custom-call(f32[8,128,512]{2,1,0:T(8,128)} %get-tuple-element.13.sums_ref, f32[8,8,128]{2,1,0:T(8,128)} %get-tuple-element.14.degree_ref, ...), custom_call_target="tpu_custom_call" | custom-call | tf_op jit(solution)/shard_map/middle/pallas_call | solution.py:342
  97.5 0.0 all-reduce.3.cloned.1.call-update
  97.6 0.0 copy-start.1
  97.6 0.0 copy-start
  97.6 6.4 %backward_terms.1.terms_ref = bf16[2,16,128,512]{3,2,1,0:T(8,128)(2,1)} custom-call(s32[1]{0:T(128)S(6)} %copy.21.count_ref, s32[1,32]{1,0:T(1,128)} %rows_ref.3, s32[1,32]{1,0:T(1,128)} %cols_ref.3, bf16[32,128,128]{2,1,0:T(8,128)(2,1)} %tiles_ref.3, bf16[8,128,512]{2,1,0:T(8,128)(2,1)} %get-tuple-element.16.agg_ref), custom_call_target="tpu_custom_call" | custom-call | tf_op jit(solution)/shard_map/backward_terms/pallas_call | solution.py:402
  104.0 37.0 %scatter_rows.1 = f32[128,512]{1,0:T(8,128)} custom-call(bf16[2,16,128,512]{3,2,1,0:T(8,128)(2,1)} %backward_terms.1.terms_ref, bf16[128,512]{1,0:T(8,128)(2,1)} %get-tuple-element.17.grad_ref, bf16[512,512]{1,0:T(8,128)(2,1)} %w_self_ref.3, s32[1,128]{1,0:T(1,128)} %order_ref.3), custom_call_target="tpu_custom_call" | custom-call | tf_op jit(solution)/shard_map/scatter_rows/pallas_call | solution.py:521
  141.0 0.0 copy-done.1
  141.0 74.6 %psum.23 = f32[512]{0:T(512)} all-reduce(f32[512]{0:T(512)S(1)} %bitcast.3), channel_id=1, replica_groups=mesh['row'=32,'col'=8] {'row','col'}, use_global_device_ids=true, to_apply=%region_2.3 | all-reduce | flops 512 | bytes 4096 | tf_op jit(solution)/shard_map/psum | solution.py:566
  215.6 146.1 %all-reduce.3.cloned.1.call-done = (f32[512,512]{1,0:T(8,128)}, f32[512,512]{1,0:T(8,128)}) async-done(((f32[512,512]{1,0:T(8,128)}, f32[512,512]{1,0:T(8,128)}), (f32[512,512]{1,0:T(8,128)}, f32[512,512]{1,0:T(8,128)})) %all-reduce.3.cloned.1.call-update) | async-done | bytes 2097168 | tf_op jit(solution)/shard_map/psum | solution.py:566
  361.7 0.0 copy-done
  361.7 0.7 copy.22
  362.4 1.7 copy.23
  364.0 2.3 copy.24
  366.3 2.3 copy.25
Async XLA Ops:
  7.2 354.5 %all-reduce.3.cloned.1.call-start = ((), (), s32[]{:S(2)}) async-start(), calls=%async_computation | async-start | bytes 4194304 | tf_op jit(solution)/shard_map/psum | solution.py:566
  97.6 43.5 %copy-start.1 = (f32[1,512]{1,0:T(1,128)S(1)}, f32[1,512]{1,0:T(1,128)}, u32[]{:S(2)}) copy-start(f32[1,512]{1,0:T(1,128)} %get-tuple-element.20) | copy-start | bytes 6148
  97.6 264.1 %copy-start = (bf16[128,512]{1,0:T(8,128)(2,1)S(1)}, bf16[128,512]{1,0:T(8,128)(2,1)}, u32[]{:S(2)}) copy-start(bf16[128,512]{1,0:T(8,128)(2,1)} %get-tuple-element.28) | copy-start | bytes 393220
Sparse Core Ops, SparseCore 0:
  97.7 263.9 all-reduce.2

commit v2 on v1

--- a/solution.py
+++ b/solution.py
@@ -12,6 +12,8 @@
 HALVES = 2
 ROWS = LINE * LINE * CORES
 COLS = LINE * HALVES
+DEPTH = LINE * HALVES
+LANES = 128
 F32 = jnp.float32
 BF16 = jnp.bfloat16
 
@@ -57,7 +59,7 @@
     return order_ref[...] == lax.broadcasted_iota(jnp.int32, (size, size), 0)
 
 
-def gather_kernel(order_ref, feat_ref, column_ref, send_sem, recv_sem, half_sem):
+def gather_kernel(order_ref, feat_ref, column_ref, own_ref, send_sem, recv_sem, half_sem):
     y, z, core = row_place()
     size = feat_ref.shape[0]
     half = size // 2
@@ -69,9 +71,11 @@
     to_along = [{"row": row_of(y, place, core)} for place in along]
     me = row_of(y, z, core)
     chosen = one_hot_order(order_ref, size).astype(F32).astype(BF16)
-    column_ref[me] = lax.dot_general(
+    own = lax.dot_general(
         chosen, feat_ref[...], (((0,), (0,)), ((), ())), preferred_element_type=F32
     ).astype(BF16)
+    own_ref[...] = own
+    column_ref[me] = own
     greet([other, to_up, to_down, *to_along])
     sent = []
 
@@ -147,9 +151,12 @@
     size, channels = features.shape
     return pl.pallas_call(
         gather_kernel,
-        out_shape=jax.ShapeDtypeStruct((ROWS, size, channels), BF16),
+        out_shape=(
+            jax.ShapeDtypeStruct((ROWS, size, channels), BF16),
+            jax.ShapeDtypeStruct((size, channels), BF16),
+        ),
         in_specs=[pl.BlockSpec(memory_space=pltpu.VMEM)] * 2,
-        out_specs=pl.BlockSpec(memory_space=pltpu.VMEM),
+        out_specs=(pl.BlockSpec(memory_space=pltpu.VMEM),) * 2,
         scratch_shapes=[
             pltpu.SemaphoreType.DMA((35,)),
             pltpu.SemaphoreType.DMA((ROWS,)),
@@ -200,10 +207,9 @@
     w_neigh_ref,
     bias_ref,
     cot_ref,
-    act_ref,
+    preact_ref,
     grad_ref,
-    self_ref,
-    neigh_ref,
+    quarter_ref,
     bias_grad_ref,
     agg_ref,
     far_out,
@@ -215,6 +221,15 @@
     mixed_in,
     cross_in,
     degree_in,
+    pair_out,
+    pair_in,
+    weight_sum,
+    weight_far,
+    weight_near,
+    weight_mixed,
+    weight_mixed_out,
+    bias_out,
+    bias_in,
     send_sem,
     far_sem,
     near_sem,
@@ -223,10 +238,15 @@
     degree_sem,
     agg_sem,
     agg_half_sem,
+    pair_sem,
+    weight_sem,
+    bias_sem,
 ):
     here = lax.axis_index("col")
     x, side = here // HALVES, here % HALVES
-    size = own_ref.shape[0]
+    size, channels = own_ref.shape
+    lanes = bias_grad_ref.shape[1]
+    quarter = quarter_ref.shape[0]
     half = size // 2
     low, high = pl.ds(0, half), pl.ds(half, half)
     up, down, far = (x + 1) % LINE, (x + LINE - 1) % LINE, (x + 2) % LINE
@@ -240,6 +260,11 @@
     to_cross = {"col": col_of(x, 1 - side)}
     peers = [to_up, to_down, to_cross, {"col": col_of(far, side)}]
     peers += [{"col": col_of(place, 1 - side)} for place in (up, down, far)]
+    y, z, core = row_place()
+    pair = {"row": row_of(y, z, 1 - core)}
+    y_up, y_down, y_far = (y + 1) % LINE, (y + LINE - 1) % LINE, (y + 2) % LINE
+    y_peers = [{"row": row_of(place, z, core)} for place in (y_up, y_down, y_far)]
+    peers += [pair, *y_peers]
     sent = []
 
     def push(source, target, recv_sem, device):
@@ -305,8 +330,20 @@
     push(agg_ref.at[here], agg_ref.at[here], agg_sem.at[here], to_up)
     push(agg_ref.at[here], agg_ref.at[here], agg_sem.at[here], to_down)
     grad_ref[...] = grad_pre
-    bent = jnp.tanh(0.5 * below)
-    act_ref[...] = (jnp.maximum(preact, 0.0) + 2.0 * bent / (1.0 - bent)).astype(BF16)
+    preact_ref[...] = preact
+    bias_part = jnp.sum(grad_pre.astype(F32), axis=0, keepdims=True)
+    bias_out[0] = jnp.zeros_like(bias_out[0])
+    for part in range(channels // lanes):
+        bias_out[0, pl.ds(part, 1)] = bias_part[:, part * lanes : (part + 1) * lanes]
+    push(bias_out.at[0], bias_in.at[0], bias_sem.at[0], pair)
+
+    def weight_part(keep):
+        left = jnp.where((core == 0) == keep, own, neigh_mean)
+        return lax.dot_general(left, grad_pre, (((0,), (0,)), ((), ())), preferred_element_type=F32)
+
+    pair_out[...] = weight_part(False)
+    push(pair_out, pair_in, pair_sem.at[0], pair)
+    weight_sum[...] = weight_part(True)
 
     def round_ring(where, slot):
         from_down, from_up = col_of(down, where), col_of(up, where)
@@ -316,20 +353,47 @@
         push(agg_ref.at[from_up, high], agg_ref.at[from_up, high], agg_half_sem.at[slot, 1], to_down)
 
     round_ring(side, 0)
-    self_ref[...] = lax.dot_general(own, grad_pre, (((0,), (0,)), ((), ())), preferred_element_type=F32)
     cross = col_of(x, 1 - side)
     arrived(agg_ref.at[cross], agg_sem.at[cross])
     push(agg_ref.at[cross], agg_ref.at[cross], agg_sem.at[cross], to_up)
     push(agg_ref.at[cross], agg_ref.at[cross], agg_sem.at[cross], to_down)
-    neigh_ref[...] = lax.dot_general(
-        neigh_mean, grad_pre, (((0,), (0,)), ((), ())), preferred_element_type=F32
-    )
-    bias_grad_ref[...] = jnp.sum(grad_pre.astype(F32), axis=0, keepdims=True)
+
+    def weight_rows(place, part):
+        return pl.ds(pl.multiple_of(place * quarter + part * (quarter // 2), 8), quarter // 2)
+
+    arrived(pair_in, pair_sem.at[0])
+    weight_sum[...] += pair_in[...]
+    for part in range(2):
+        push(weight_sum.at[weight_rows(y_far, part)], weight_far.at[part], weight_sem.at[0, part], y_peers[part])
+    near_rows = (weight_rows(y_up, 1), weight_rows(y_down, 0))
+    for part in range(2):
+        push(weight_sum.at[near_rows[part]], weight_near.at[part], weight_sem.at[1, part], y_peers[part])
+    arrived(bias_in.at[0], bias_sem.at[0])
+    bias_out[1] = bias_out[0] + bias_in[0]
+    for offset, device in enumerate(y_peers):
+        push(bias_out.at[1], bias_in.at[1 + offset], bias_sem.at[1 + offset], device)
     round_ring(1 - side, 1)
+    mixed_rows = (weight_rows(y_up, 0), weight_rows(y_down, 1))
+    for part in range(2):
+        arrived(weight_far.at[part], weight_sem.at[0, part])
+        weight_mixed_out[part] = weight_sum[mixed_rows[part]] + weight_far[part]
+        push(weight_mixed_out.at[part], weight_mixed.at[part], weight_sem.at[2, part], y_peers[part])
+    bias_total = bias_out[1]
+    for offset in range(LINE - 1):
+        arrived(bias_in.at[1 + offset], bias_sem.at[1 + offset])
+        bias_total += bias_in[1 + offset]
+    bias_grad_ref[...] = bias_total
     for slot, where in enumerate((side, 1 - side)):
         block = col_of(far, where)
         arrived(agg_ref.at[block, low], agg_half_sem.at[slot, 0])
         arrived(agg_ref.at[block, high], agg_half_sem.at[slot, 1])
+    for part in range(2):
+        arrived(weight_near.at[part], weight_sem.at[1, part])
+        arrived(weight_mixed.at[part], weight_sem.at[2, part])
+    for part in range(2):
+        quarter_ref[pl.ds(part * (quarter // 2), quarter // 2)] = (
+            weight_sum[weight_rows(y, part)] + weight_mixed[part] + weight_near[1 - part]
+        )
     for copy in sent:
         copy.wait_send()
 
@@ -338,19 +402,19 @@
     size, channels = own.shape
     half = size // 2
     wide = w_self.shape[0]
+    eighth = wide // (2 * LINE)
     halves = functools.partial(pltpu.VMEM, dtype=BF16)
     return pl.pallas_call(
         middle_kernel,
         out_shape=(
+            jax.ShapeDtypeStruct((size, channels), F32),
             jax.ShapeDtypeStruct((size, channels), BF16),
-            jax.ShapeDtypeStruct((size, channels), BF16),
-            jax.ShapeDtypeStruct((wide, wide), F32),
-            jax.ShapeDtypeStruct((wide, wide), F32),
-            jax.ShapeDtypeStruct((1, wide), F32),
+            jax.ShapeDtypeStruct((wide // LINE, wide), F32),
+            jax.ShapeDtypeStruct((8, LANES), F32),
             jax.ShapeDtypeStruct((COLS, size, channels), BF16),
         ),
         in_specs=[pl.BlockSpec(memory_space=pltpu.VMEM)] * 7,
-        out_specs=(pl.BlockSpec(memory_space=pltpu.VMEM),) * 6,
+        out_specs=(pl.BlockSpec(memory_space=pltpu.VMEM),) * 5,
         scratch_shapes=[
             halves((2, size, channels)),
             halves((2, 2, half, channels)),
@@ -361,7 +425,16 @@
             halves((2, 2, half, channels)),
             halves((size, channels)),
             pltpu.VMEM((COLS, 8, size), F32),
-            pltpu.SemaphoreType.DMA((30,)),
+            pltpu.VMEM((wide, wide), F32),
+            pltpu.VMEM((wide, wide), F32),
+            pltpu.VMEM((wide, wide), F32),
+            pltpu.VMEM((2, eighth, wide), F32),
+            pltpu.VMEM((2, eighth, wide), F32),
+            pltpu.VMEM((2, eighth, wide), F32),
+            pltpu.VMEM((2, eighth, wide), F32),
+            pltpu.VMEM((2, 8, LANES), F32),
+            pltpu.VMEM((LINE, 8, LANES), F32),
+            pltpu.SemaphoreType.DMA((40,)),
             pltpu.SemaphoreType.DMA((2, 2)),
             pltpu.SemaphoreType.DMA((2, 2)),
             pltpu.SemaphoreType.DMA((2, 2)),
@@ -369,13 +442,16 @@
             pltpu.SemaphoreType.DMA((COLS,)),
             pltpu.SemaphoreType.DMA((COLS,)),
             pltpu.SemaphoreType.DMA((2, 2)),
+            pltpu.SemaphoreType.DMA((1,)),
+            pltpu.SemaphoreType.DMA((3, 2)),
+            pltpu.SemaphoreType.DMA((LINE,)),
         ],
         compiler_params=pltpu.CompilerParams(collective_id=1, has_side_effects=True),
         name="middle",
     )(sums, degree, own, w_self, w_neigh, bias, cotangent)
 
 
-def backward_kernel(count_ref, rows_ref, cols_ref, tiles_ref, agg_ref, terms_ref, total):
+def backward_kernel(count_ref, rows_ref, cols_ref, tiles_ref, agg_ref, preact_ref, terms_ref, act_ref, total):
     total[...] = jnp.zeros_like(total)
 
     def advance(slot, carry):
@@ -395,26 +471,35 @@
         return carry
 
     lax.fori_loop(0, ROWS, put, 0)
-
-
-def backward_terms(count, rows_at, cols_at, tiles, agg):
+    preact = preact_ref[...]
+    bent = jnp.tanh(0.5 * jnp.minimum(preact, 0.0))
+    act_ref[...] = (jnp.maximum(preact, 0.0) + 2.0 * bent / (1.0 - bent)).astype(BF16)
+
+
+def backward_terms(count, rows_at, cols_at, tiles, agg, preact):
     _, size, channels = agg.shape
     return pl.pallas_call(
         backward_kernel,
-        out_shape=jax.ShapeDtypeStruct((CORES, ROWS // CORES, size, channels), BF16),
-        in_specs=[pl.BlockSpec(memory_space=pltpu.SMEM)] * 3 + [pl.BlockSpec(memory_space=pltpu.VMEM)] * 2,
-        out_specs=pl.BlockSpec(memory_space=pltpu.VMEM),
+        out_shape=(
+            jax.ShapeDtypeStruct((CORES, ROWS // CORES, size, channels), BF16),
+            jax.ShapeDtypeStruct((size, channels), BF16),
+        ),
+        in_specs=[pl.BlockSpec(memory_space=pltpu.SMEM)] * 3 + [pl.BlockSpec(memory_space=pltpu.VMEM)] * 3,
+        out_specs=(pl.BlockSpec(memory_space=pltpu.VMEM),) * 2,
         scratch_shapes=[pltpu.VMEM((ROWS, size, channels), F32)],
         name="backward_terms",
-    )(count, rows_at, cols_at, tiles, agg)
+    )(count, rows_at, cols_at, tiles, agg, preact)
 
 
 def scatter_kernel(
     terms_ref,
     grad_ref,
     w_self_ref,
-    order_ref,
+    quarter_ref,
+    bias_ref,
     out_ref,
+    weights_ref,
+    bias_grad_ref,
     pair_in,
     far_out,
     near_out,
@@ -424,12 +509,25 @@
     near_in,
     mixed_in,
     line_in,
+    x_in,
+    z_out,
+    z_in,
+    bias_out,
+    bias_in,
     send_sem,
     pair_sem,
     far_sem,
     near_sem,
     mixed_sem,
     line_sem,
+    x_sem,
+    z_sem,
+    bias_sem,
+    deep_sem,
+    ring_sem,
+    wide_sem,
+    wide_half_sem,
+    both_sem,
 ):
     y, z, core = row_place()
     size = grad_ref.shape[0]
@@ -447,7 +545,93 @@
     def push(source, target, recv_sem, device):
         sent.append(start_copy(source, target, send_sem.at[len(sent)], recv_sem, device))
 
-    greet([other, to_up, to_down, *to_along])
+    here = lax.axis_index("col")
+    x, side = here // HALVES, here % HALVES
+    deep = side * LINE + z
+    x_up, x_down, x_far = (x + 1) % LINE, (x + LINE - 1) % LINE, (x + 2) % LINE
+
+    def at_x(place):
+        return {"col": place * HALVES + side}
+
+    def at_deep(place):
+        return {"row": row_of(y, place % LINE, core), "col": x * HALVES + place // LINE}
+
+    y_peers = [to_up, to_down, {"row": row_of(far, z, core)}]
+    deep_peers = [(deep + offset) % DEPTH for offset in range(1, DEPTH)]
+    greet([other, *y_peers, *(at_deep(place) for place in deep_peers), at_x(x_up), at_x(x_down), at_x(x_far)])
+
+    strip = x_in.shape[1]
+    for offset in range(1, LINE):
+        place = (x + offset) % LINE
+        rows = pl.ds(pl.multiple_of(place * strip, 8), strip)
+        push(quarter_ref.at[rows], x_in.at[offset], x_sem.at[offset], at_x(place))
+        push(bias_ref, bias_in.at[offset], bias_sem.at[offset], at_x(place))
+
+    def reduced_x():
+        mine = quarter_ref[pl.ds(pl.multiple_of(x * strip, 8), strip)]
+        bias = bias_ref[...]
+        for offset in range(1, LINE):
+            arrived(x_in.at[offset], x_sem.at[offset])
+            mine += x_in[offset]
+            arrived(bias_in.at[offset], bias_sem.at[offset])
+            bias += bias_in[offset]
+        low_rows = strip // 2
+        for place in range(DEPTH):
+            rows = slice((place % 2) * low_rows, (place % 2 + 1) * low_rows)
+            z_out[place] = mine[rows, (place // 2) * LANES : (place // 2 + 1) * LANES]
+        bias_out[...] = bias
+        for offset, place in enumerate(deep_peers, 1):
+            push(z_out.at[place], z_in.at[offset], z_sem.at[offset], at_deep(place))
+            push(bias_out, bias_in.at[LINE + offset], bias_sem.at[LINE + offset], at_deep(place))
+
+    def reduced_z():
+        mine = z_out[deep]
+        bias = bias_out[...]
+        for offset in range(1, DEPTH):
+            arrived(z_in.at[offset], z_sem.at[offset])
+            mine += z_in[offset]
+            arrived(bias_in.at[LINE + offset], bias_sem.at[LINE + offset])
+            bias += bias_in[LINE + offset]
+        bias_grad_ref[...] = bias
+        piece = weights_ref.at[core, x, y, deep]
+        weights_ref[core, x, y, deep] = mine
+        for place in deep_peers:
+            push(piece, piece, deep_sem.at[deep], at_deep(place))
+
+    def gathered_z():
+        for place in deep_peers:
+            arrived(weights_ref.at[core, x, y, place], deep_sem.at[place])
+        piece = weights_ref.at[core, x, y]
+        for device in y_peers:
+            push(piece, piece, ring_sem.at[y], device)
+
+    def both_cores(place):
+        piece = weights_ref.at[core, place]
+        push(piece, piece, both_sem.at[place], other)
+
+    def gathered_y():
+        for place in (up, down, far):
+            arrived(weights_ref.at[core, x, place], ring_sem.at[place])
+        piece = weights_ref.at[core, x]
+        push(piece, piece, wide_sem.at[x], at_x(x_up))
+        push(piece, piece, wide_sem.at[x], at_x(x_down))
+        both_cores(x)
+
+    def gathered_near_x():
+        for part, (source, target) in enumerate(((x_down, x_up), (x_up, x_down))):
+            arrived(weights_ref.at[core, source], wide_sem.at[source])
+            piece = weights_ref.at[core, source, pl.ds(part * (LINE // 2), LINE // 2)]
+            push(piece, piece, wide_half_sem.at[part], at_x(target))
+            both_cores(source)
+
+    def gathered_x():
+        for part in range(2):
+            piece = weights_ref.at[core, x_far, pl.ds(part * (LINE // 2), LINE // 2)]
+            arrived(piece, wide_half_sem.at[part])
+        both_cores(x_far)
+        for place in range(LINE):
+            arrived(weights_ref.at[1 - core, place], both_sem.at[place])
+
     for ring in (far, up, down, y):
         for place in places:
             block = ring * LINE + place
@@ -467,7 +651,12 @@
         far_out[index] = paired(far, place, everything).astype(BF16)
         push(far_out.at[index, low], far_in.at[index, 0], far_sem.at[index, 0], to_up)
         push(far_out.at[index, high], far_in.at[index, 1], far_sem.at[index, 1], to_down)
+    reduced_x()
     for index, place in enumerate(places):
+        if index == 2:
+            reduced_z()
+        if index == LINE - 1:
+            gathered_z()
         wait_pair(up, place)
         near_out[index, 0] = paired(up, place, high).astype(BF16)
         push(near_out.at[index, 0], near_in.at[index, 0], near_sem.at[index, 0], to_up)
@@ -498,31 +687,34 @@
     for index in range(LINE - 1):
         line_out[index] = gathered(index).astype(BF16)
         push(line_out.at[index], line_in.at[index], line_sem.at[index], to_along[LINE - 2 - index])
+        if index == 1:
+            gathered_y()
     local += gathered(LINE - 1)
+    gathered_near_x()
     for index in range(LINE - 1):
         arrived(line_in.at[index], line_sem.at[index])
         local += line_in[index].astype(F32)
-    chosen = one_hot_order(order_ref, size).astype(F32).astype(BF16)
-    moved = jnp.zeros_like(local)
-    rest = local
-    for _ in range(3):
-        piece = rest.astype(BF16)
-        moved += jnp.dot(chosen, piece, preferred_element_type=F32)
-        rest -= piece.astype(F32)
-    out_ref[...] = moved
+    out_ref[...] = local
+    gathered_x()
     for copy in sent:
         copy.wait_send()
 
 
-def scatter_rows(terms, grad_pre, w_self, order):
+def scatter_rows(terms, grad_pre, w_self, quarter, bias):
     size, channels = grad_pre.shape
     half = size // 2
+    strip = quarter.shape[0] // LINE
+    piece = (strip // 2, LANES)
     halves = functools.partial(pltpu.VMEM, dtype=BF16)
     return pl.pallas_call(
         scatter_kernel,
-        out_shape=jax.ShapeDtypeStruct((size, channels), F32),
-        in_specs=[pl.BlockSpec(memory_space=pltpu.VMEM)] * 4,
-        out_specs=pl.BlockSpec(memory_space=pltpu.VMEM),
+        out_shape=(
+            jax.ShapeDtypeStruct((size, channels), F32),
+            jax.ShapeDtypeStruct((CORES, LINE, LINE, DEPTH, *piece), F32),
+            jax.ShapeDtypeStruct(bias.shape, F32),
+        ),
+        in_specs=[pl.BlockSpec(memory_space=pltpu.VMEM)] * 5,
+        out_specs=(pl.BlockSpec(memory_space=pltpu.VMEM),) * 3,
         scratch_shapes=[
             halves((LINE * LINE, size, channels)),
             halves((LINE, size, channels)),
@@ -533,16 +725,70 @@
             halves((LINE, 2, half, channels)),
             halves((LINE, 2, half, channels)),
             halves((LINE - 1, size, channels)),
-            pltpu.SemaphoreType.DMA((43,)),
+            pltpu.VMEM((LINE, strip, quarter.shape[1]), F32),
+            pltpu.VMEM((DEPTH, *piece), F32),
+            pltpu.VMEM((DEPTH, *piece), F32),
+            pltpu.VMEM(bias.shape, F32),
+            pltpu.VMEM((LINE + DEPTH, *bias.shape), F32),
+            pltpu.SemaphoreType.DMA((90,)),
             pltpu.SemaphoreType.DMA((LINE * LINE,)),
             pltpu.SemaphoreType.DMA((LINE, 2)),
             pltpu.SemaphoreType.DMA((LINE, 2)),
             pltpu.SemaphoreType.DMA((LINE, 2)),
             pltpu.SemaphoreType.DMA((LINE - 1,)),
+            pltpu.SemaphoreType.DMA((LINE,)),
+            pltpu.SemaphoreType.DMA((DEPTH,)),
+            pltpu.SemaphoreType.DMA((LINE + DEPTH,)),
+            pltpu.SemaphoreType.DMA((DEPTH,)),
+            pltpu.SemaphoreType.DMA((LINE,)),
+            pltpu.SemaphoreType.DMA((LINE,)),
+            pltpu.SemaphoreType.DMA((2,)),
+            pltpu.SemaphoreType.DMA((LINE,)),
         ],
         compiler_params=pltpu.CompilerParams(collective_id=2, has_side_effects=True),
         name="scatter_rows",
-    )(terms, grad_pre, w_self, order)
+    )(terms, grad_pre, w_self, quarter, bias)
+
+
+def finish_kernel(order_ref, local_ref, weights_ref, bias_ref, feature_ref, self_ref, neigh_ref, bias_grad_ref):
+    size = local_ref.shape[0]
+    chosen = one_hot_order(order_ref, size).astype(F32).astype(BF16)
+    rest = local_ref[...]
+    moved = jnp.zeros_like(rest)
+    for _ in range(3):
+        piece = rest.astype(BF16)
+        moved += jnp.dot(chosen, piece, preferred_element_type=F32)
+        rest -= piece.astype(F32)
+    feature_ref[...] = moved
+    low_rows = weights_ref.shape[4]
+
+    def put(index, carry):
+        x, y = index // LINE, index % LINE
+        for core, target in enumerate((self_ref, neigh_ref)):
+            for place in range(DEPTH):
+                row = pl.multiple_of((y * LINE + x) * 2 * low_rows + (place % 2) * low_rows, 8)
+                target[pl.ds(row, low_rows), pl.ds((place // 2) * LANES, LANES)] = weights_ref[core, x, y, place]
+        return carry
+
+    lax.fori_loop(0, LINE * LINE, put, 0)
+    for part in range(bias_grad_ref.shape[1] // LANES):
+        bias_grad_ref[:, pl.ds(part * LANES, LANES)] = bias_ref[pl.ds(part, 1)]
+
+
+def finish(order, local, weights, bias):
+    wide = local.shape[1]
+    return pl.pallas_call(
+        finish_kernel,
+        out_shape=(
+            jax.ShapeDtypeStruct(local.shape, F32),
+            jax.ShapeDtypeStruct((wide, wide), F32),
+            jax.ShapeDtypeStruct((wide, wide), F32),
+            jax.ShapeDtypeStruct((1, wide), F32),
+        ),
+        in_specs=[pl.BlockSpec(memory_space=pltpu.VMEM)] * 4,
+        out_specs=(pl.BlockSpec(memory_space=pltpu.VMEM),) * 4,
+        name="finish",
+    )(order, local, weights, bias)
 
 
 def shards(
@@ -557,15 +803,14 @@
     bias_term,
     cotangent,
 ):
-    column = gather_rows(node_order, features)
-    own = lax.dynamic_index_in_dim(column, lax.axis_index("row"), 0, keepdims=False)
+    column, own = gather_rows(node_order, features)
     sums, degree = forward_sums(tile_count, tile_rows, tile_cols, edge_tiles, column)
-    activations, grad_pre, self_part, neigh_part, bias_part, agg = middle(
+    preact, grad_pre, quarter, bias_part, agg = middle(
         sums, degree, own, w_self, w_neigh, bias_term[None], cotangent
     )
-    self_grad, neigh_grad, bias_grad = lax.psum((self_part, neigh_part, bias_part), ("row", "col"))
-    terms = backward_terms(tile_count, tile_rows, tile_cols, edge_tiles, agg)
-    feature_grad = scatter_rows(terms, grad_pre, w_self, node_order)
+    terms, activations = backward_terms(tile_count, tile_rows, tile_cols, edge_tiles, agg, preact)
+    local, weights, bias_sum = scatter_rows(terms, grad_pre, w_self, quarter, bias_part)
+    feature_grad, self_grad, neigh_grad, bias_grad = finish(node_order, local, weights, bias_sum)
     return (activations, feature_grad, self_grad, neigh_grad, bias_grad[0])
 
 

time: 376 us -> 151 us (0.40)
  waiting for transfers between devices: 146 us -> 0 us
  blocking collectives: 74.6 us -> 0 us
  Pallas kernels: 130 us -> 146 us
  between operations: 14.7 us -> 1.3 us
  local copies, waits for them, and re-layouts: 9.69 us -> 1.26 us
    psum x1 -> x0, waiting for transfers between devices: 146 us -> none  [shards(): lax.psum((self_part, neigh_part, bias_part), ('row', 'col'))]
    psum x1 -> x0, blocking collectives: 74.6 us -> none  [shards(): lax.psum((self_part, neigh_part, bias_part), ('row', 'col'))]
    pallas_call x3 -> x4, Pallas kernels: 78.1 us -> 90.3 us  [the longest x1 42.7 us: scatter_rows(): pl.pallas_call(scatter_kernel, out_shape=(jax.ShapeDtypeStruct((size, cha...]
    unnamed x8 -> x0, local copies, waits for them, and re-layouts: 6.86 us -> none
  transfers between devices with their start and end apart: 1 -> 0, of which waited for: 1 -> 0; matrix products, arithmetic and copies ran while one was open for 0% -> 0% of each run, Pallas kernels for 12% -> 0%
where the time goes in v2:
time: 151 us; the launch traced here: 149 us
  Pallas kernels  146 us (97%)
    pallas_call x1, Pallas kernels, middle(): pl.pallas_call(middle_kernel, out_shape=(jax.ShapeDtypeStruct((size, chan...  48.1 us
    pallas_call x1, Pallas kernels, scatter_rows(): pl.pallas_call(scatter_kernel, out_shape=(jax.ShapeDtypeStruct((size, cha...  42.7 us
    pallas_call x1, Pallas kernels, gather_rows(): pl.pallas_call(gather_kernel, out_shape=(jax.ShapeDtypeStruct((ROWS, size...  34.7 us
    pallas_call x1, Pallas kernels, backward_terms(): pl.pallas_call(backward_kernel, out_shape=(jax.ShapeDtypeStruct((CORES, R...  9.23 us
    pallas_call x1, Pallas kernels, forward_sums(): pl.pallas_call(forward_kernel, out_shape=(jax.ShapeDtypeStruct((COLS, siz...  7.91 us
    pallas_call x1, Pallas kernels, finish(): pl.pallas_call(finish_kernel, out_shape=(jax.ShapeDtypeStruct(local.shape...  3.68 us

profile of v2, /device:TPU:2, one launch (start us, length us, event | category | flops | bytes accessed | tf_op | source)
XLA Modules:
  0.0 148.9 jit_solution(7216167446406646912)
XLA Ops:
  1.3 1.3 broadcast_in_dim.3.bias_ref
  2.5 34.7 %gather_rows.1 = (bf16[32,128,512]{2,1,0:T(8,128)(2,1)}, bf16[128,512]{1,0:T(8,128)(2,1)}) custom-call(s32[1,128]{1,0:T(1,128)} %order_ref.3, bf16[128,512]{1,0:T(8,128)(2,1)} %feat_ref.1), custom_call_target="tpu_custom_call" | custom-call | tf_op jit(solution)/shard_map/gather_rows/pallas_call | solution.py:152
  37.3 7.9 %forward_sums.1 = (f32[8,128,512]{2,1,0:T(8,128)}, f32[8,8,128]{2,1,0:T(8,128)}) custom-call(s32[1]{0:T(128)S(6)} %copy.15.count_ref, s32[1,32]{1,0:T(1,128)} %rows_ref.3, s32[1,32]{1,0:T(1,128)} %cols_ref.3, bf16[32,128,128]{2,1,0:T(8,128)(2,1)} %tiles_ref.3, bf16[32,128,512]{2,1,0:T(8,128)(2,1)} %get-tuple-element.23.column_ref), custom_call_target="tpu_custom_call" | custom-call | tf_op jit(solution)/shard_map/forward_sums/pallas_call | solution.py:190
  45.2 48.1 %middle.1 = (f32[128,512]{1,0:T(8,128)}, bf16[128,512]{1,0:T(8,128)(2,1)}, f32[128,512]{1,0:T(8,128)}, f32[8,128]{1,0:T(8,128)}, bf16[8,128,512]{2,1,0:T(8,128)(2,1)}) custom-call(f32[8,128,512]{2,1,0:T(8,128)} %get-tuple-element.24.sums_ref, f32[8,8,128]{2,1,0:T(8,128)} %get-tuple-element.25.degree_ref, bf16[128,512]{1,0:T(8,128)(2,1)} %get-tuple-element.26.own_ref, ...), custom_call_target="tpu_custom_call" | custom-call | tf_op jit(solution)/shard_map/middle/pallas_call | solution.py:407
  93.3 9.2 %backward_terms.1 = (bf16[2,16,128,512]{3,2,1,0:T(8,128)(2,1)}, bf16[128,512]{1,0:T(8,128)(2,1)}) custom-call(s32[1]{0:T(128)S(6)} %copy.15.count_ref, s32[1,32]{1,0:T(1,128)} %rows_ref.3, s32[1,32]{1,0:T(1,128)} %cols_ref.3, bf16[32,128,128]{2,1,0:T(8,128)(2,1)} %tiles_ref.3, bf16[8,128,512]{2,1,0:T(8,128)(2,1)} %get-tuple-element.27.agg_ref, ...), custom_call_target="tpu_custom_call" | custom-call | tf_op jit(solution)/shard_map/backward_terms/pallas_call | solution.py:481
  102.5 42.7 %scatter_rows.1 = (f32[128,512]{1,0:T(8,128)}, f32[2,4,4,8,16,128]{5,4,3,2,1,0:T(8,128)}, f32[8,128]{1,0:T(8,128)}) custom-call(bf16[2,16,128,512]{3,2,1,0:T(8,128)(2,1)} %get-tuple-element.30.terms_ref, bf16[128,512]{1,0:T(8,128)(2,1)} %get-tuple-element.31.grad_ref, bf16[512,512]{1,0:T(8,128)(2,1)} %w_self_ref.3, ...), custom_call_target="tpu_custom_call" | custom-call | tf_op jit(solution)/shard_map/scatter_rows/pallas_call | solution.py:709
  145.2 3.7 %finish.1 = (f32[128,512]{1,0:T(8,128)}, f32[512,512]{1,0:T(8,128)}, f32[512,512]{1,0:T(8,128)}, f32[1,512]{1,0:T(1,128)}) custom-call(s32[1,128]{1,0:T(1,128)} %order_ref.3, f32[128,512]{1,0:T(8,128)} %get-tuple-element.34.local_ref, f32[2,4,4,8,16,128]{5,4,3,2,1,0:T(8,128)} %get-tuple-element.35.weights_ref, f32[8,128]{1,0:T(8,128)} %get-tuple-element.36.bias_ref), custom_call_target="tpu_custom_call" | custom-call | tf_op jit(solution)/shard_map/finish/pallas_call | solution.py:780
